TPU v7x, 256 devices: a whole 4x4x8 slice. The times are simulated.
256 devices in a mesh: dp: 8 (over x, core), mp: 32 (over y, z).
Axes of the slice: x: 4, y: 4, z: 8, core: 2. Of those that a mesh axis runs over, the one named last changes fastest.
Arguments:
- hidden: bfloat16 [4096, 4096], P('dp'), may hold values from -170 to 170
- encoded: bfloat16 [64, 114688], P('dp'), may hold values from -4 to 4
- neighbours: int32 [64, 2], P('dp'), may hold values from 0 to 63, as said below
- w_query: bfloat16 [4096, 4096], P(None, 'mp'), as said below
- w_key: bfloat16 [896, 4096], P(None, 'mp'), as said below
- w_value: bfloat16 [896, 4096], P(None, 'mp'), may hold values from -0.1875 to 0.1875
- w_out: bfloat16 [4096, 4096], P('mp'), may hold values from -0.1875 to 0.1875
- cotangent: bfloat16 [4096, 4096], P('dp'), may hold values from -16 to 16
Outputs:
- attended: bfloat16 [4096, 4096], P('dp', 'mp')
- grad_hidden: bfloat16 [4096, 4096], P('dp', 'mp')
- grad_encoded: bfloat16 [64, 114688], P('dp', 'mp')
Inputs may be any that keep to these rules, and one draw needn't show every extreme that they name: `neighbours`: an id is owner * 8 + slot: the neighbour is row slot of the rows of encoded held by dp index owner. Of the 16 ids of one index of dp, at most 4 name one owner; one owner, the same for every index, is named exactly 4 times by every index of dp. `w_query`: entries scaled by the inverse square root of 4096. `w_key`: entries scaled by the inverse square root of 896, or smaller.
All inputs are finite; a program needn't handle non-finite values.
Results may differ from a plain program's by a relative error of at most 0.0065.
The roundings to bfloat16 on the way count: a program that leaves them out, or rounds other values in their place, can miss the bound.
Values may be sent and summed in bfloat16 or wider, within the bound.
No kernel may reach another device: no remote copies, remote signals or barrier semaphores. Data moves between devices by JAX's collectives and lax.ppermute only.
A program may use at most 128 MiB of HBM per device.

v0:
```python
import math

import jax
import jax.numpy as jnp
from jax import lax
from jax.sharding import PartitionSpec as P

DH = 128


def shards(hidden, encoded, neighbours, w_query, w_key, w_value, w_out, cotangent):
    tok_rows = hidden.shape[0]
    owners = lax.axis_size("dp")
    blocks = neighbours.shape[0]
    per_block = neighbours.shape[1]
    requests = blocks * per_block
    capacity = requests // 4
    block_len = tok_rows // blocks
    stored = encoded.shape[0]
    enc_width = w_key.shape[0]
    seg_len = encoded.shape[1] // enc_width
    head_cols = w_query.shape[1]
    head_dim = DH
    heads_here = head_cols // head_dim
    inv_root = 1.0 / math.sqrt(head_dim)
    flat_ids = neighbours.reshape(requests)
    owner_of = flat_ids // stored
    slot_of = flat_ids % stored
    owner_mask = (owner_of[:, None] == jnp.arange(owners)[None, :]).astype(jnp.int32)
    position = jnp.sum(jnp.cumsum(owner_mask, axis=0) * owner_mask, axis=1) - 1
    target = owner_of * capacity + position
    placed = target[:, None] == jnp.arange(owners * capacity)[None, :]
    send_ids = (jnp.sum(jnp.where(placed, slot_of[:, None] + 1, 0), axis=0) - 1).reshape(
        owners, capacity
    )
    w_pair = jnp.concatenate([w_key, w_value], axis=1)
    queries = jnp.dot(hidden, w_query, preferred_element_type=jnp.float32).astype(jnp.bfloat16)
    ids_piece = lax.all_to_all(send_ids, "dp", split_axis=0, concat_axis=0, tiled=True)
    gathered = jnp.take(encoded, jnp.maximum(ids_piece, 0), axis=0)
    arrived = lax.all_to_all(gathered, "dp", split_axis=0, concat_axis=0, tiled=True)
    arrived = arrived.reshape(owners * capacity, arrived.shape[-1])
    picked = jnp.take(arrived, target, axis=0)
    fetched = jnp.dot(
        picked.reshape(requests * seg_len, enc_width), w_pair, preferred_element_type=jnp.float32
    )
    fetched = fetched.astype(jnp.bfloat16).reshape(requests, seg_len, 2 * head_cols)
    keys_all = fetched.reshape(blocks, per_block * seg_len, 2, heads_here, head_dim)
    ctx_keys = keys_all[:, :, 0]
    ctx_values = keys_all[:, :, 1]
    q_blocks = queries.reshape(blocks, block_len, heads_here, head_dim)
    scores = (
        jnp.einsum("cqhd,ckhd->chqk", q_blocks, ctx_keys, preferred_element_type=jnp.float32)
        * inv_root
    )
    row_max = jnp.max(scores, axis=-1, keepdims=True)
    exp_terms = jnp.exp(scores - row_max)
    prob_full = exp_terms / jnp.sum(exp_terms, axis=-1, keepdims=True)
    prob_half = prob_full.astype(jnp.bfloat16)
    attn_out = jnp.einsum(
        "chqk,ckhd->cqhd", prob_half, ctx_values, preferred_element_type=jnp.float32
    ).astype(jnp.bfloat16)
    attn_flat = attn_out.reshape(tok_rows, head_cols)
    partial_value = jnp.dot(attn_flat, w_out, preferred_element_type=jnp.float32)
    attended = lax.psum_scatter(partial_value, "mp", scatter_dimension=1, tiled=True).astype(
        jnp.bfloat16
    )
    grad_attn = lax.dot_general(
        cotangent, w_out, (((1,), (1,)), ((), ())), preferred_element_type=jnp.float32
    ).astype(jnp.bfloat16)
    grad_blocks = grad_attn.reshape(blocks, block_len, heads_here, head_dim)
    grad_prob = jnp.einsum(
        "cqhd,ckhd->chqk", grad_blocks, ctx_values, preferred_element_type=jnp.float32
    )
    grad_values = jnp.einsum(
        "chqk,cqhd->ckhd", prob_half, grad_blocks, preferred_element_type=jnp.float32
    ).astype(jnp.bfloat16)
    grad_scores = (
        prob_full * (grad_prob - jnp.sum(prob_full * grad_prob, axis=-1, keepdims=True))
    ).astype(jnp.bfloat16)
    grad_query = (
        jnp.einsum("chqk,ckhd->cqhd", grad_scores, ctx_keys, preferred_element_type=jnp.float32)
        * inv_root
    ).astype(jnp.bfloat16)
    grad_keys = (
        jnp.einsum("chqk,cqhd->ckhd", grad_scores, q_blocks, preferred_element_type=jnp.float32)
        * inv_root
    ).astype(jnp.bfloat16)
    grad_pair = jnp.stack([grad_keys, grad_values], axis=2).reshape(
        requests, seg_len * 2 * head_cols
    )
    outgoing = (
        jnp.zeros((owners * capacity, seg_len * 2 * head_cols), jnp.bfloat16)
        .at[target]
        .set(grad_pair)
    )
    returned = lax.all_to_all(
        outgoing.reshape(owners, capacity, seg_len * 2 * head_cols),
        "dp",
        split_axis=0,
        concat_axis=0,
        tiled=True,
    )
    gradq_flat = grad_query.reshape(tok_rows, head_cols)
    returned = returned.reshape(owners * capacity, seg_len * 2 * head_cols)
    slot_hits = (jnp.arange(stored)[:, None] == ids_piece.reshape(1, owners * capacity)).astype(
        jnp.bfloat16
    )
    grad_stored = jnp.dot(slot_hits, returned, preferred_element_type=jnp.float32).astype(
        jnp.bfloat16
    )
    grad_stored = grad_stored.reshape(stored * seg_len, 2 * head_cols)
    enc_terms = lax.dot_general(
        grad_stored, w_pair, (((1,), (1,)), ((), ())), preferred_element_type=jnp.float32
    )
    enc_terms = enc_terms.reshape(stored, seg_len * enc_width)
    grad_terms = lax.dot_general(
        gradq_flat, w_query, (((1,), (1,)), ((), ())), preferred_element_type=jnp.float32
    )
    grad_hidden, grad_encoded = (
        lax.psum_scatter(grad_terms, "mp", scatter_dimension=1, tiled=True),
        lax.psum_scatter(enc_terms, "mp", scatter_dimension=1, tiled=True),
    )
    return (attended, grad_hidden.astype(jnp.bfloat16), grad_encoded.astype(jnp.bfloat16))


def solution(mesh):
    placed = (
        P("dp", None),
        P("dp", None),
        P("dp", None),
        P(None, "mp"),
        P(None, "mp"),
        P(None, "mp"),
        P("mp", None),
        P("dp", None),
    )
    return jax.shard_map(
        shards,
        mesh=mesh,
        in_specs=placed,
        out_specs=(P("dp", "mp"), P("dp", "mp"), P("dp", "mp")),
        check_vma=False,
    )
```

profile of v0, /device:TPU:32, one launch (start us, length us, event | category | flops | bytes accessed | tf_op | source)
XLA Modules:
  0.0 916.0 jit_solution(10768926833555992109)
XLA Ops:
  8.7 9.4 %all_to_all.16 = s32[8,1,4]{2,1,0:T(1,128)S(1)} all-to-all(s32[8,1,4]{2,1,0:T(1,128)S(1)} %bitcast.71), channel_id=1, replica_groups=mesh['dp'=8,'mp'=32] {'dp'}, dimensions={0} | all-to-all | bytes 256 | tf_op jit(solution)/shard_map/all_to_all | solution.py:38
  19.3 8.4 gather_fusion
  27.7 7.6 reshape.310
  35.5 9.3 %broadcast_select_fusion = bf16[8,4,114688]{2,1,0:T(4,128)(2,1)} fusion(bf16[8,4,114688]{2,1,0:T(4,128)(2,1)} %reshape.310, pred[8,4]{1,0:T(8,128)(4,1)S(1)} %copy.35), kind=kLoop, calls=%fused_computation.5 | loop fusion | flops 3670016 | bytes 14680096 | tf_op jit(solution)/shard_map/jit(_take)/select_n | solution.py:39
  44.8 5.2 all-to-all-start.1
  50.3 3.6 convolution_convert_fusion.4
  53.9 1.3 convolution_convert_fusion.3
  55.2 78.0 %all-to-all-done.1 = bf16[8,4,114688]{2,1,0:T(4,128)(2,1)} async-done(((bf16[8,4,114688]{2,1,0:T(4,128)(2,1)}), bf16[8,4,114688]{2,1,0:T(4,128)(2,1)}, u32[]{:S(2)}, u32[]{:S(2)}) %all-to-all-start.1) | async-done | bytes 7340064 | tf_op jit(solution)/shard_map/all_to_all | solution.py:40
  133.2 7.2 reshape.296
  140.4 11.8 %gather_fusion.1 = bf16[16,114688]{1,0:T(8,128)(2,1)} fusion(bf16[32,114688]{1,0:T(8,128)(2,1)} %reshape.296, s32[1024]{0:T(1024)S(1)} %pad_clamp_fusion), kind=kCustom, calls=%fused_computation.1 | custom fusion | bytes 7340096 | tf_op jit(solution)/shard_map/jit(_take)/gather | solution.py:42
  152.2 4.5 gather.12
  156.6 3.4 fusion.4
  160.3 1.7 fusion.25
  163.3 1.4 fusion.26
  164.7 1.9 fusion.11
  169.4 3.6 scatter_custom_fusion
  173.0 4.1 reshape.305
  177.1 4.3 all-to-all-start.2
  181.6 27.1 %all-to-all-done.2 = bf16[8,4,32768]{2,1,0:T(4,128)(2,1)} async-done(((bf16[8,4,32768]{2,1,0:T(4,128)(2,1)}), bf16[8,4,32768]{2,1,0:T(4,128)(2,1)}, u32[]{:S(2)}, u32[]{:S(2)}) %all-to-all-start.2) | async-done | bytes 2097184 | tf_op jit(solution)/shard_map/all_to_all | solution.py:96
  208.6 4.0 reshape.306
  212.6 2.0 convolution_convert_fusion
  214.9 2.5 fusion.29
  217.4 4.5 reshape.308
  222.0 1.1 copy-done.3
  223.4 4.5 fusion.28
  230.1 4.5 fusion.27
  234.6 208.0 %reduce-scatter.8.cloned.1.call-done = f32[8,3584]{1,0:T(8,128)} async-done(((f32[8,114688]{1,0:T(8,128)}), f32[8,3584]{1,0:T(8,128)}) %reduce-scatter.8.cloned.1.call-update) | async-done | bytes 114704 | tf_op jit(solution)/shard_map/reduce_scatter | solution.py:121
  442.6 1.5 convert_element_type.90
  444.2 231.4 %reduce-scatter.6.cloned.1.call-done = f32[512,128]{1,0:T(8,128)} async-done(((f32[512,4096]{1,0:T(8,128)}), f32[512,128]{1,0:T(8,128)}) %reduce-scatter.6.cloned.1.call-update) | async-done | bytes 262160 | tf_op jit(solution)/shard_map/reduce_scatter | solution.py:120
  675.6 1.6 convert_element_type.82
  677.2 230.7 %reduce-scatter.4.cloned.1.call-done = f32[512,128]{1,0:T(8,128)} async-done(((f32[512,4096]{1,0:T(8,128)}), f32[512,128]{1,0:T(8,128)}) %reduce-scatter.4.cloned.1.call-update) | async-done | bytes 262160 | tf_op jit(solution)/shard_map/reduce_scatter | solution.py:64
  907.9 1.6 convert_element_type.76
  (68 shorter events, 10.5 us)
Async XLA Ops:
  7.2 12.1 %copy-start = (bf16[8,114688]{1,0:T(8,128)(2,1)S(1)}, bf16[8,114688]{1,0:T(8,128)(2,1)}, u32[]{:S(2)}) copy-start(bf16[8,114688]{1,0:T(8,128)(2,1)} %param.9) | copy-start | bytes 5505028
  44.8 5.3 copy-start.11
  44.8 5.4 copy-start.12
  44.8 5.5 copy-start.8
  44.8 88.4 %all-to-all-start.1 = ((bf16[8,4,114688]{2,1,0:T(4,128)(2,1)}), bf16[8,4,114688]{2,1,0:T(4,128)(2,1)}, u32[]{:S(2)}, u32[]{:S(2)}) async-start(bf16[8,4,114688]{2,1,0:T(4,128)(2,1)} %broadcast_select_fusion), calls=%async_computation.1 | async-start | bytes 14680064 | tf_op jit(solution)/shard_map/all_to_all | solution.py:40
  50.0 3.9 copy-start.4
  50.1 3.9 copy-start.13
  162.0 1.0 copy-start.2
  162.0 5.2 copy-start.6
  166.6 1.0 copy-start.10
  177.1 31.5 %all-to-all-start.2 = ((bf16[8,4,32768]{2,1,0:T(4,128)(2,1)}), bf16[8,4,32768]{2,1,0:T(4,128)(2,1)}, u32[]{:S(2)}, u32[]{:S(2)}) async-start(bf16[8,4,32768]{2,1,0:T(4,128)(2,1)} %reshape.305), calls=%async_computation.4 | async-start | bytes 4194304 | tf_op jit(solution)/shard_map/all_to_all | solution.py:96
  181.4 261.2 %reduce-scatter.8.cloned.1.call-start = ((), (), s32[]{:S(2)}) async-start(), calls=%async_computation.8 | async-start | bytes 3784704 | tf_op jit(solution)/shard_map/reduce_scatter | solution.py:121
  221.9 1.2 copy-start.3
  221.9 1.5 copy-start.9
  221.9 453.6 %reduce-scatter.6.cloned.1.call-start = ((), (), s32[]{:S(2)}) async-start(), calls=%async_computation.7 | async-start | bytes 8650752 | tf_op jit(solution)/shard_map/reduce_scatter | solution.py:120
  227.9 1.2 copy-start.7
  227.9 2.2 copy-start.5
  227.9 679.9 %reduce-scatter.4.cloned.1.call-start = ((), (), s32[]{:S(2)}) async-start(), calls=%async_computation.6 | async-start | bytes 8650752 | tf_op jit(solution)/shard_map/reduce_scatter | solution.py:64
  234.6 674.9 %copy-start.1 = (bf16[8,114688]{1,0:T(8,128)(2,1)S(1)}, bf16[8,114688]{1,0:T(8,128)(2,1)}, u32[]{:S(2)}) copy-start(bf16[8,114688]{1,0:T(8,128)(2,1)} %param.9) | copy-start | bytes 5505028
Sparse Core Ops, SparseCore 0:
  222.0 220.5 reduce-scatter.7
  447.2 228.3 reduce-scatter.5
  679.6 228.2 reduce-scatter.3
where the time goes:
time: 918 us; the launch traced here: 916 us
  waiting for transfers between devices  775 us (84%)
  local copies, waits for them, and re-layouts  65.1 us (7%)
  matrix products  25.8 us (3%)
  other arithmetic  16.9 us (2%)
  between operations  14 us (2%)
  starting transfers between devices  9.62 us (1%)
  blocking collectives  9.36 us (1%)
    reduce_scatter x1, waiting for transfers between devices, shards(): lax.psum_scatter(grad_terms, 'mp', scatter_dimension=1, tiled=True)  231 us
    reduce_scatter x1, waiting for transfers between devices, shards(): lax.psum_scatter(partial_value, 'mp', scatter_dimension=1, tiled=True)  231 us
    reduce_scatter x1, waiting for transfers between devices, shards(): lax.psum_scatter(enc_terms, 'mp', scatter_dimension=1, tiled=True)  208 us
    all_to_all x1, waiting for transfers between devices, shards(): lax.all_to_all(gathered, 'dp', split_axis=0, concat_axis=0, tiled=True)  78 us
    all_to_all x1, waiting for transfers between devices, shards(): lax.all_to_all(outgoing.reshape(owners, capacity, seg_len * 2 * head_cols...  27.1 us
  transfers between devices with their start and end apart: 5, of which 5 were waited for; matrix products, arithmetic and copies ran while one was open for 2% of the time, Pallas kernels for 0%

commit v1 on v0

v1 whole, which is shorter than its diff:
```python
import functools
import math

import jax
import jax.numpy as jnp
from jax import lax
from jax.experimental import pallas as pl
from jax.experimental.pallas import tpu as pltpu
from jax.sharding import Mesh, PartitionSpec as P

DH = 128
BF = jnp.bfloat16
F32 = jnp.float32
NT = (((1,), (1,)), ((), ()))
TN = (((0,), (0,)), ((), ()))
VMEM_LIMIT = 48 * 1024 * 1024


def params():
    return pltpu.CompilerParams(vmem_limit_bytes=VMEM_LIMIT)


def call(body, out_shape, n_scalar, n_in, flops, moved, scratch=()):
    single = not isinstance(out_shape, (tuple, list))
    n_out = 1 if single else len(out_shape)
    vmem = pl.BlockSpec(memory_space=pltpu.VMEM)
    smem = pl.BlockSpec(memory_space=pltpu.SMEM)
    return pl.pallas_call(
        body,
        out_shape=out_shape,
        in_specs=[smem] * n_scalar + [vmem] * n_in,
        out_specs=vmem if single else (vmem,) * n_out,
        scratch_shapes=list(scratch),
        compiler_params=params(),
        cost_estimate=pl.CostEstimate(flops=flops, bytes_accessed=moved, transcendentals=0),
    )


def attention_body(geom, pos_ref, ids_ref, q_ref, g_ref, *refs):
    blocks, block_len, n_x, n_y, cap, stored = geom
    kv_refs, (attn_ref, gq_ref, out_ref, kv_ref) = refs[:-4], refs[-4:]
    near, far = kv_refs[:6], kv_refs[6:]
    inv_root = 1.0 / math.sqrt(DH)
    seg = kv_ref.shape[1]
    piece = seg // n_y
    half = stored // 2
    my_x, my_c = pos_ref[0], pos_ref[1]
    requests = 2 * blocks
    out_ref[...] = jnp.zeros_like(out_ref)
    ids = [ids_ref[r // 2, r % 2] for r in range(requests)]
    owners = [i // stored for i in ids]
    for r in range(requests):
        slot = ids[r] % stored
        dx = lax.rem(owners[r] // 2 - my_x + n_x, n_x)
        dc = lax.rem(owners[r] % 2 + my_c, 2)
        which = dc * n_x + dx
        for c in range(2):
            for j, d in enumerate((0, 1, 3)):

                @pl.when(which == c * n_x + d)
                def _(r=r, ref=near[c * 3 + j], slot=slot):
                    kv_ref[r] = ref[slot]

            for h in range(2):

                @pl.when((which == c * n_x + 2) & (slot // half == h))
                def _(r=r, ref=far[c * 2 + h], slot=slot):
                    kv_ref[r] = ref[lax.rem(slot, half)]

    for c in range(blocks):
        k = kv_ref[2 * c : 2 * c + 2, :, :DH].reshape(2 * seg, DH)
        v = kv_ref[2 * c : 2 * c + 2, :, DH:].reshape(2 * seg, DH)
        rows = slice(c * block_len, (c + 1) * block_len)
        q = q_ref[rows, :]
        g = g_ref[rows, :]
        s = lax.dot_general(q, k, NT, preferred_element_type=F32) * inv_root
        e = jnp.exp(s - jnp.max(s, axis=-1, keepdims=True))
        p = e / jnp.sum(e, axis=-1, keepdims=True)
        ph = p.astype(BF)
        gp = lax.dot_general(g, v, NT, preferred_element_type=F32)
        attn_ref[rows, :] = jnp.dot(ph, v, preferred_element_type=F32).astype(BF)
        gs = (p * (gp - jnp.sum(p * gp, axis=-1, keepdims=True))).astype(BF)
        gq_ref[rows, :] = (jnp.dot(gs, k, preferred_element_type=F32) * inv_root).astype(BF)
        gv = lax.dot_general(ph, g, TN, preferred_element_type=F32).astype(BF)
        gk = (lax.dot_general(gs, q, TN, preferred_element_type=F32) * inv_root).astype(BF)
        for j in range(2):
            r = 2 * c + j
            pos = sum([(owners[i] == owners[r]).astype(jnp.int32) for i in range(r)], jnp.int32(0))
            for y in range(n_y):
                part = slice(j * seg + y * piece, j * seg + (y + 1) * piece)
                out_ref[owners[r], y, pos, :, :DH] = gk[part, :]
                out_ref[owners[r], y, pos, :, DH:] = gv[part, :]


def encoded_body(stored, pos_ref, ids_ref, ret_ref, w_ref, out_ref, acc_ref, prod_ref):
    owners, n_y, cap, piece, _ = ret_ref.shape
    me = pos_ref[0] * 2 + pos_ref[1]
    blocks = ids_ref.shape[0] // owners
    acc_ref[...] = jnp.zeros_like(acc_ref)

    def from_device(d, carry):
        count = jnp.int32(0)
        for r in range(2 * blocks):
            at = ids_ref[d * blocks + r // 2, r % 2]
            named = at // stored == me

            @pl.when(named)
            def _(at=at, count=count):
                slot = lax.rem(at, stored)
                for y in range(n_y):
                    acc_ref[y, slot] += ret_ref[d, y, count].astype(F32)

            count = count + named.astype(jnp.int32)
        return carry

    lax.fori_loop(0, owners, from_device, 0)
    lanes = prod_ref.shape[0]
    for y in range(n_y):
        both = acc_ref[y].astype(BF).reshape(stored * piece, 2 * DH)
        for n in range(lanes):
            w = w_ref[y, n * DH : (n + 1) * DH, :]
            term = lax.dot_general(both, w, NT, preferred_element_type=F32)
            prod_ref[n] = term if y == 0 else prod_ref[n] + term
    for t in range(0, piece, 2):
        for n in range(lanes):
            two = [prod_ref[n, pl.ds(t + k, stored, stride=piece), :] for k in range(2)]
            out_ref[pl.ds(t * stored, 2 * stored), n * DH : (n + 1) * DH] = jnp.concatenate(two, axis=0).astype(BF)


def head_sum_body(n_z, n_y, second, pos_ref, *refs):
    pieces, (mine_ref, other_ref), outs = refs[:n_z], refs[n_z : n_z + 2], refs[n_z + 2 :]
    my_c, my_y, my_z = pos_ref[1], pos_ref[2], pos_ref[3]

    def with_weights(w_ref):
        for k in range(0, n_y, 2):
            total = None
            for j in range(n_z):
                src = lax.rem(my_z + j, n_z)
                w = [w_ref[src, lax.rem(my_y + k + i, n_y)] for i in range(2)]
                if second:
                    w = jnp.concatenate(w, axis=0)
                    term = lax.dot_general(pieces[j][...], w, NT, preferred_element_type=F32)
                else:
                    w = jnp.concatenate(w, axis=1)
                    term = jnp.dot(pieces[j][...], w, preferred_element_type=F32)
                total = term if total is None else total + term
            for i in range(2):
                outs[k + i][...] = total[:, i * DH : (i + 1) * DH].astype(outs[k + i].dtype)

    @pl.when(my_c == second)
    def _():
        with_weights(mine_ref)

    @pl.when(my_c != second)
    def _():
        with_weights(other_ref)


def shards(hidden, encoded, neighbours, w_query, w_key, w_value, w_out, cotangent):
    n_x, n_c, n_y, n_z = (lax.axis_size(a) for a in ("x", "c", "y", "z"))
    dp = ("x", "c")
    owners = n_x * n_c
    rows, width = hidden.shape
    blocks, per_block = neighbours.shape
    cap = blocks * per_block // 4
    stored = encoded.shape[0]
    enc_width = w_key.shape[0]
    seg = encoded.shape[1] // enc_width
    block_len = rows // blocks
    piece = seg // n_y
    core = lax.axis_index("c")
    place = jnp.stack([lax.axis_index(a) for a in ("x", "c", "y", "z")]).astype(jnp.int32)

    def shift(axis, n, k):
        return lambda a: lax.ppermute(a, axis, [(i, (i + k) % n) for i in range(n)])

    swap = shift("c", n_c, 1)
    x_up, x_down = shift("x", n_x, -1), shift("x", n_x, 1)
    z_up, z_down = shift("z", n_z, -1), shift("z", n_z, 1)

    w_pair = jnp.concatenate([w_key, w_value], axis=1)
    enc_rows = encoded.reshape(stored, seg, enc_width).transpose(1, 0, 2).reshape(seg * stored, enc_width)
    kv = jnp.dot(enc_rows, w_pair, preferred_element_type=F32).astype(BF)
    kv = kv.reshape(seg, stored, 2 * DH).transpose(1, 0, 2)
    after, before = x_up(kv), x_down(kv)
    half = stored // 2
    far = [x_up(after[:half]), x_down(before[half:])]
    near = [kv, after, before]
    kv_all = near + [swap(a) for a in near] + far + [swap(a) for a in far]

    w_query_, w_out_, w_pair_, hidden_, cotangent_, neighbours_, kv_ = lax.optimization_barrier(
        (w_query, w_out, w_pair, hidden, cotangent, neighbours, kv)
    )
    wo_blocks = w_out_.reshape(DH, n_y, n_z, DH).transpose(2, 1, 0, 3)
    wq_blocks = w_query_.reshape(n_y, n_z, DH, DH).transpose(1, 0, 2, 3)
    mine = jnp.where(core == 0, wo_blocks, wq_blocks)
    mine = lax.all_to_all(mine, "z", 0, 0, tiled=True)
    other = swap(mine)
    pair_all = lax.all_gather(w_pair, "y")
    ids_all = lax.all_gather(neighbours_, dp, tiled=True)

    queries = jnp.dot(hidden_, w_query_, preferred_element_type=F32).astype(BF)
    grad_attn = lax.dot_general(cotangent_, w_out_, NT, preferred_element_type=F32).astype(BF)

    slab = jax.ShapeDtypeStruct((rows, DH), BF)
    attn, gq, outgoing = call(
        functools.partial(attention_body, (blocks, block_len, n_x, n_y, cap, stored)),
        (slab, slab, jax.ShapeDtypeStruct((owners, n_y, cap, piece, 2 * DH), BF)),
        2, 2 + len(kv_all), 500_000_000, 5 << 20,
        scratch=(pltpu.VMEM((blocks * per_block, seg, 2 * DH), BF),),
    )(place, neighbours, queries, grad_attn, *kv_all)

    returned = lax.all_to_all(
        outgoing.reshape(owners * n_y, cap, piece, 2 * DH), dp + ("y",), 0, 0, tiled=True
    ).reshape(owners, n_y, cap, piece, 2 * DH)
    enc_part = call(
        functools.partial(encoded_body, stored),
        jax.ShapeDtypeStruct((piece * stored, enc_width), BF), 2, 2, 500_000_000, 5 << 20,
        scratch=(
            pltpu.VMEM((n_y, stored, piece, 2 * DH), F32),
            pltpu.VMEM((enc_width // DH, stored * piece, DH), F32),
        ),
    )(place, ids_all, returned, pair_all)
    enc_parts = lax.all_to_all(enc_part.reshape(n_z, -1, enc_width), "z", 0, 0, tiled=True)
    enc_rows_sum = jnp.sum(enc_parts.astype(F32), axis=0).astype(BF)
    grad_encoded = enc_rows_sum.reshape(seg // (n_y * n_z), stored, enc_width).transpose(1, 0, 2).reshape(stored, -1)

    def ring(own):
        pieces = {0: own}
        for k in range(1, n_z // 2 + 1):
            pieces[k] = z_up(pieces[k - 1])
        last = own
        for k in range(1, n_z - n_z // 2):
            last = z_down(last)
            pieces[n_z - k] = last
        return [pieces[k] for k in range(n_z)]

    def summed(own, second):
        parts = call(
            functools.partial(head_sum_body, n_z, n_y, second),
            (jax.ShapeDtypeStruct((rows, DH), F32),) + (slab,) * (n_y - 1),
            1, n_z + 2, 540_000_000, 3 << 20,
        )(place, *ring(own), mine, other)
        total = parts[0]
        for k in range(1, n_y):
            total = total + shift("y", n_y, k)(parts[k]).astype(F32)
        return total.astype(BF)

    return summed(attn, 0), summed(gq, 1), grad_encoded


def solution(mesh):
    n_y = 4
    dp, mp = mesh.shape["dp"], mesh.shape["mp"]
    split = Mesh(mesh.devices.reshape(dp // 2, 2, n_y, mp // n_y), ("x", "c", "y", "z"))
    d, m = ("x", "c"), ("y", "z")
    return jax.shard_map(
        shards,
        mesh=split,
        in_specs=(P(d, None), P(d, None), P(d, None), P(None, m), P(None, m), P(None, m), P(m, None), P(d, None)),
        out_specs=(P(d, m), P(d, m), P(d, m)),
        check_vma=False,
    )
```

time: 918 us -> 169 us (0.18)
  waiting for transfers between devices: 775 us -> 32.7 us
  local copies, waits for them, and re-layouts: 65.1 us -> 15.1 us
  starting transfers between devices: 9.62 us -> 55.5 us
  Pallas kernels: 0 us -> 19.6 us
  matrix products: 25.8 us -> 8.27 us
  other arithmetic: 16.9 us -> 5.54 us
    reduce_scatter x3 -> x0, waiting for transfers between devices: 670 us -> none  [the longest x1 231 us: shards(): lax.psum_scatter(grad_terms, 'mp', scatter_dimension=1, tiled=True)]
    all_to_all x2 -> x3, waiting for transfers between devices: 105 us -> 0.01 us  [the longest x1 0.01 us: shards(): lax.all_to_all(outgoing.reshape(owners * n_y, cap, piece, 2 * DH), dp + (...]
    ppermute x0 -> x30, starting transfers between devices: none -> 34.3 us  [shift(): return lambda a: lax.ppermute(a, axis, [(i, (i + k) % n) for i in range(n)])]
    ppermute x0 -> x30, waiting for transfers between devices: none -> 32.7 us  [shift(): return lambda a: lax.ppermute(a, axis, [(i, (i + k) % n) for i in range(n)])]
    gather x4 -> x0, local copies, waits for them, and re-layouts: 32.2 us -> none  [the longest x2 16.2 us: shards(): picked = jnp.take(arrived, target, axis=0)]
    pallas_call x0 -> x4, Pallas kernels: none -> 19.6 us  [the longest x1 8.01 us: shards(): call(functools.partial(attention_body, (blocks, block_len, n_x, n_y, cap,...]
    reshape x8 -> x2, local copies, waits for them, and re-layouts: 21 us -> 1.72 us  [the longest x1 1.62 us: shards(): wo_blocks = w_out_.reshape(DH, n_y, n_z, DH).transpose(2, 1, 0, 3)]
    dot_general x13 -> x3, matrix products: 25.8 us -> 8.27 us  [the longest x1 3.78 us: shards(): queries = jnp.dot(hidden_, w_query_, preferred_element_type=F32).astype(BF)]
  transfers between devices with their start and end apart: 5 -> 34, of which waited for: 5 -> 10; matrix products, arithmetic and copies ran while one was open for 2% -> 8% of each run, Pallas kernels for 0% -> 12%
where the time goes in v1:
time: 169 us; the launch traced here: 166 us
  starting transfers between devices  55.5 us (33%)
  waiting for transfers between devices  32.7 us (19%)
  Pallas kernels  19.6 us (12%)
  local copies, waits for them, and re-layouts  15.1 us (9%)
  blocking collectives  14.7 us (9%)
  between operations  14.2 us (8%)
  matrix products  8.27 us (5%)
  other arithmetic  5.54 us (3%)
    ppermute x30, starting transfers between devices, shift(): return lambda a: lax.ppermute(a, axis, [(i, (i + k) % n) for i in range(n)])  34.3 us
    ppermute x30, waiting for transfers between devices, shift(): return lambda a: lax.ppermute(a, axis, [(i, (i + k) % n) for i in range(n)])  32.7 us
    all_gather x1, blocking collectives, shards(): ids_all = lax.all_gather(neighbours_, dp, tiled=True)  14.7 us
    all_to_all x1, starting transfers between devices, shards(): mine = lax.all_to_all(mine, 'z', 0, 0, tiled=True)  8.7 us
    pallas_call x1, Pallas kernels, shards(): call(functools.partial(attention_body, (blocks, block_len, n_x, n_y, cap,...  8.01 us
    all_to_all x1, starting transfers between devices, shards(): lax.all_to_all(enc_part.reshape(n_z, -1, enc_width), 'z', 0, 0, tiled=True)  7.21 us
    unnamed x23, local copies, waits for them, and re-layouts  6.52 us
    pallas_call x1, Pallas kernels, shards(): call(functools.partial(encoded_body, stored), jax.ShapeDtypeStruct((piece...  6.24 us
  transfers between devices with their start and end apart: 34, of which 10 were waited for; matrix products, arithmetic and copies ran while one was open for 8% of the time, Pallas kernels for 12%

profile of v1, /device:TPU:32, one launch (start us, length us, event | category | flops | bytes accessed | tf_op | source)
XLA Modules:
  0.0 165.6 jit_solution(17004210390320884682)
XLA Ops:
  11.2 2.3 %copy.25 = bf16[128,4096]{0,1:T(8,128)(2,1)} copy(bf16[128,4096]{1,0:T(8,128)(2,1)} %param.14) | data formatting | bytes 2097152 | tf_op jit(solution)/shard_map/optimization_barrier | solution.py:191
  13.5 1.6 copy.26
  15.1 2.3 %bitcast_select_fusion = bf16[8,4,128,128]{3,2,1,0:T(8,128)(2,1)} fusion(bf16[128,4,8,128]{3,0,1,2:T(8,128)(2,1)S(1)} %copy.26, bf16[4,8,128,128]{3,2,1,0:T(8,128)(2,1)} %bitcast.48, pred[]{:T(512)S(6)} %eq.3), kind=kLoop, calls=%fused_computation.4 | loop fusion | flops 524288 | bytes 3145729 | tf_op jit(solution)/shard_map/jit(_where)/select_n | solution.py:196
  17.4 8.7 %all-to-all-start = ((bf16[8,4,128,128]{3,2,1,0:T(8,128)(2,1)}), bf16[8,4,128,128]{3,2,1,0:T(8,128)(2,1)S(1)}, u32[]{:S(2)}, u32[]{:S(2)}) async-start(bf16[8,4,128,128]{3,2,1,0:T(8,128)(2,1)} %bitcast_select_fusion), calls=%async_computation | async-start | bytes 2097152 | tf_op jit(solution)/shard_map/all_to_all | solution.py:197
  26.2 2.8 %collective-permute-start = (bf16[8,128,256]{2,1,0:T(8,128)(2,1)S(1)}, bf16[8,128,256]{2,1,0:T(8,128)(2,1)}, u32[]{:S(2)}, u32[]{:S(2)}) collective-permute-start(bf16[8,128,256]{2,1,0:T(8,128)(2,1)S(1)} %bitcast.39), channel_id=1, source_target_pairs={{0,192},{64,0},{128,64},{192,128},{1,193},{65,1},{129,65},{193,129... | collective-permute-start | bytes 1572872 | tf_op jit(solution)/shard_map/ppermute | solution.py:175
  28.9 10.6 %collective-permute-done.refs_1_ = bf16[8,128,256]{2,1,0:T(8,128)(2,1)} collective-permute-done((bf16[8,128,256]{2,1,0:T(8,128)(2,1)S(1)}, bf16[8,128,256]{2,1,0:T(8,128)(2,1)}, u32[]{:S(2)}, u32[]{:S(2)}) %collective-permute-start) | collective-permute-done | bytes 524320 | tf_op jit(solution)/shard_map/ppermute | solution.py:175
  39.5 1.7 %slice.8 = bf16[4,128,256]{2,1,0:T(8,128)(2,1)} slice(bf16[8,128,256]{2,1,0:T(8,128)(2,1)} %collective-permute-done.refs_1_), slice={[0:4], [0:128], [0:256]} | slice | bytes 524288 | tf_op jit(solution)/shard_map/slice | solution.py:187
  41.2 3.8 %collective-permute-start.5 = (bf16[4,128,256]{2,1,0:T(8,128)(2,1)}, bf16[4,128,256]{2,1,0:T(8,128)(2,1)}, u32[]{:S(2)}, u32[]{:S(2)}) collective-permute-start(bf16[4,128,256]{2,1,0:T(8,128)(2,1)} %slice.8), channel_id=1, source_target_pairs={{0,192},{64,0},{128,64},{192,128},{1,193},{65,1},{129,65},{193,129... | collective-permute-start | bytes 786440 | tf_op jit(solution)/shard_map/ppermute | solution.py:175
  45.0 1.7 %slice.9 = bf16[4,128,256]{2,1,0:T(8,128)(2,1)} slice(bf16[8,128,256]{2,1,0:T(8,128)(2,1)} %collective-permute-done.1.refs_2_), slice={[4:8], [0:128], [0:256]} | slice | bytes 524288 | tf_op jit(solution)/shard_map/slice | solution.py:187
  47.2 3.7 %convolution_convert_fusion.1.g_ref = bf16[512,128]{1,0:T(8,128)(2,1)S(1)} fusion(bf16[512,4096]{1,0:T(8,128)(2,1)} %param.15, bf16[128,4096]{1,0:T(8,128)(2,1)} %param.14), kind=kOutput, calls=%fused_computation.2 | convolution fusion | flops 536936448 | bytes 5373952 | tf_op jit(solution)/shard_map/dot_general | solution.py:203
  51.2 3.4 %collective-permute-done.6.refs_7_ = bf16[4,128,256]{2,1,0:T(8,128)(2,1)} collective-permute-done((bf16[4,128,256]{2,1,0:T(8,128)(2,1)}, bf16[4,128,256]{2,1,0:T(8,128)(2,1)}, u32[]{:S(2)}, u32[]{:S(2)}) %collective-permute-start.6) | collective-permute-done | bytes 262176 | tf_op jit(solution)/shard_map/ppermute | solution.py:175
  54.6 3.8 %convolution_convert_fusion.2.q_ref = bf16[512,128]{1,0:T(8,128)(2,1)S(1)} fusion(bf16[512,4096]{1,0:T(8,128)(2,1)} %param.8, bf16[4096,128]{1,0:T(8,128)(2,1)} %param.11), kind=kOutput, calls=%fused_computation.3 | convolution fusion | flops 536936448 | bytes 5373952 | tf_op jit(solution)/shard_map/dot_general | solution.py:202
  58.4 8.0 %shard_map.103 = (bf16[512,128]{1,0:T(8,128)(2,1)S(1)}, bf16[512,128]{1,0:T(8,128)(2,1)S(1)}, bf16[8,4,4,32,256]{4,3,2,1,0:T(8,128)(2,1)}) custom-call(s32[4]{0:T(128)S(1)} %pad_add_fusion.pos_ref, s32[8,2]{1,0:T(8,128)S(1)} %copy.24.ids_ref, bf16[512,128]{1,0:T(8,128)(2,1)S(1)} %convolution_convert_fusion.2.q_ref, ...), custom_call_target="tpu_custom_call" | custom-call | flops 500000000 | bytes 5242880 | tf_op jit(solution)/shard_map/pallas_call | solution.py:206
  67.8 5.2 %all-to-all-start.1 = ((bf16[32,4,32,256]{3,2,1,0:T(8,128)(2,1)}), bf16[32,4,32,256]{3,2,1,0:T(8,128)(2,1)}, u32[]{:S(2)}, u32[]{:S(2)}) async-start(bf16[32,4,32,256]{3,2,1,0:T(8,128)(2,1)} %bitcast.46), calls=%async_computation.1 | async-start | bytes 4194304 | tf_op jit(solution)/shard_map/all_to_all | solution.py:213
  73.9 2.6 %collective-permute-start.9 = (bf16[512,128]{1,0:T(8,128)(2,1)S(1)}, bf16[512,128]{1,0:T(8,128)(2,1)S(1)}, u32[]{:S(2)}, u32[]{:S(2)}) collective-permute-start(bf16[512,128]{1,0:T(8,128)(2,1)S(1)} %copy-done.3), channel_id=1, source_target_pairs={{0,7},{1,0},{2,1},{3,2},{4,3},{5,4},{6,5},{7,6},{8,15},{9,8},{10,9... | collective-permute-start | bytes 393224 | tf_op jit(solution)/shard_map/ppermute | solution.py:175
  76.5 3.0 %collective-permute-done.20.refs_1_ = bf16[512,128]{1,0:T(8,128)(2,1)S(1)} collective-permute-done((bf16[512,128]{1,0:T(8,128)(2,1)S(1)}, bf16[512,128]{1,0:T(8,128)(2,1)S(1)}, u32[]{:S(2)}, u32[]{:S(2)}) %collective-permute-start.20) | collective-permute-done | bytes 131104 | tf_op jit(solution)/shard_map/ppermute | solution.py:175
  82.3 2.4 %collective-permute-start.10 = (bf16[512,128]{1,0:T(8,128)(2,1)S(1)}, bf16[512,128]{1,0:T(8,128)(2,1)}, u32[]{:S(2)}, u32[]{:S(2)}) collective-permute-start(bf16[512,128]{1,0:T(8,128)(2,1)S(1)} %collective-permute-done.9.refs_1_), channel_id=1, source_target_pairs={{0,7},{1,0},{2,1},{3,2},{4,3},{5,4},{6,5},{7,6},{8,15},{9,8},{10,9... | collective-permute-start | bytes 393224 | tf_op jit(solution)/shard_map/ppermute | solution.py:175
  85.3 2.7 %collective-permute-start.22 = (bf16[512,128]{1,0:T(8,128)(2,1)}, bf16[512,128]{1,0:T(8,128)(2,1)}, u32[]{:S(2)}, u32[]{:S(2)}) collective-permute-start(bf16[512,128]{1,0:T(8,128)(2,1)} %collective-permute-done.21.refs_2_), channel_id=1, source_target_pairs={{0,7},{1,0},{2,1},{3,2},{4,3},{5,4},{6,5},{7,6},{8,15},{9,8},{10,9... | collective-permute-start | bytes 393224 | tf_op jit(solution)/shard_map/ppermute | solution.py:175
  88.0 14.7 %all-gather.1 = s32[8,8,2]{1,2,0:T(2,128)S(1)} all-gather(s32[1,8,2]{1,2,0:T(2,128)S(1)} %bitcast.50), channel_id=1, replica_groups=mesh['x'=4,'c'=2,'y'=4,'z'=8] {'x','c'}, dimensions={0}, use_global_device_ids=true | all-gather | bytes 576 | tf_op jit(solution)/shard_map/all_gather | solution.py:200
  102.9 1.5 copy-done.1
  104.4 6.2 %shard_map.106 = bf16[256,896]{1,0:T(8,128)(2,1)} custom-call(s32[4]{0:T(128)S(1)} %pad_add_fusion.pos_ref, s32[64,2]{1,0:T(8,128)S(1)} %bitcast.44, bf16[8,4,4,32,256]{4,3,2,1,0:T(8,128)(2,1)} %bitcast.17.ret_ref, bf16[4,896,256]{2,1,0:T(8,128)(2,1)S(1)} %bitcast.43), custom_call_target="tpu_custom_call" | custom-call | flops 500000000 | bytes 5242880 | tf_op jit(solution)/shard_map/pallas_call | solution.py:216
  110.6 7.2 %all-to-all-start.2 = ((bf16[8,32,896]{2,1,0:T(8,128)(2,1)}), bf16[8,32,896]{2,1,0:T(8,128)(2,1)}, u32[]{:S(2)}, u32[]{:S(2)}) async-start(bf16[8,32,896]{2,1,0:T(8,128)(2,1)} %bitcast.19), calls=%async_computation.2 | async-start | bytes 917504 | tf_op jit(solution)/shard_map/all_to_all | solution.py:224
  117.9 1.5 collective-permute-start.14
  121.9 10.2 %collective-permute-done.14.refs_6_ = bf16[512,128]{1,0:T(8,128)(2,1)S(1)} collective-permute-done((bf16[512,128]{1,0:T(8,128)(2,1)S(1)}, bf16[512,128]{1,0:T(8,128)(2,1)S(1)}, u32[]{:S(2)}, u32[]{:S(2)}) %collective-permute-start.14) | collective-permute-done | bytes 131104 | tf_op jit(solution)/shard_map/ppermute | solution.py:175
  133.5 2.0 %collective-permute-start.12 = (bf16[512,128]{1,0:T(8,128)(2,1)S(1)}, bf16[512,128]{1,0:T(8,128)(2,1)S(1)}, u32[]{:S(2)}, u32[]{:S(2)}) collective-permute-start(bf16[512,128]{1,0:T(8,128)(2,1)S(1)} %collective-permute-done.11.refs_3_), channel_id=1, source_target_pairs={{0,7},{1,0},{2,1},{3,2},{4,3},{5,4},{6,5},{7,6},{8,15},{9,8},{10,9... | collective-permute-start | bytes 393224 | tf_op jit(solution)/shard_map/ppermute | solution.py:175
  136.8 2.8 %shard_map.105 = (f32[512,128]{1,0:T(8,128)S(1)}, bf16[512,128]{1,0:T(8,128)(2,1)S(1)}, bf16[512,128]{1,0:T(8,128)(2,1)S(1)}, bf16[512,128]{1,0:T(8,128)(2,1)S(1)}) custom-call(s32[4]{0:T(128)S(1)} %pad_add_fusion.pos_ref, bf16[512,128]{1,0:T(8,128)(2,1)S(1)} %copy-done.5, bf16[512,128]{1,0:T(8,128)(2,1)S(1)} %copy-done.7, ...), custom_call_target="tpu_custom_call" | custom-call | flops 540000000 | bytes 3145728 | tf_op jit(solution)/shard_map/pallas_call | solution.py:239
  139.6 1.7 %collective-permute-start.27 = (bf16[512,128]{1,0:T(8,128)(2,1)S(1)}, bf16[512,128]{1,0:T(8,128)(2,1)S(1)}, u32[]{:S(2)}, u32[]{:S(2)}) collective-permute-start(bf16[512,128]{1,0:T(8,128)(2,1)S(1)} %get-tuple-element.30), channel_id=1, source_target_pairs={{0,8},{8,16},{16,24},{24,0},{1,9},{9,17},{17,25},{25,1},{2,10},{10... | collective-permute-start | bytes 393224 | tf_op jit(solution)/shard_map/ppermute | solution.py:175
  141.3 3.1 %collective-permute-start.28 = (bf16[512,128]{1,0:T(8,128)(2,1)S(1)}, bf16[512,128]{1,0:T(8,128)(2,1)S(1)}, u32[]{:S(2)}, u32[]{:S(2)}) collective-permute-start(bf16[512,128]{1,0:T(8,128)(2,1)S(1)} %get-tuple-element.31), channel_id=1, source_target_pairs={{0,16},{8,24},{16,0},{24,8},{1,17},{9,25},{17,1},{25,9},{2,18},{10... | collective-permute-start | bytes 393224 | tf_op jit(solution)/shard_map/ppermute | solution.py:175
  145.3 2.6 %shard_map.104 = (f32[512,128]{1,0:T(8,128)S(1)}, bf16[512,128]{1,0:T(8,128)(2,1)S(1)}, bf16[512,128]{1,0:T(8,128)(2,1)S(1)}, bf16[512,128]{1,0:T(8,128)(2,1)S(1)}) custom-call(s32[4]{0:T(128)S(1)} %pad_add_fusion.pos_ref, bf16[512,128]{1,0:T(8,128)(2,1)S(1)} %copy-done.3, bf16[512,128]{1,0:T(8,128)(2,1)S(1)} %collective-permute-done.9.refs_1_, ...), custom_call_target="tpu_custom_call" | custom-call | flops 540000000 | bytes 3145728 | tf_op jit(solution)/shard_map/pallas_call | solution.py:239
  149.5 2.3 %collective-permute-start.19 = (bf16[512,128]{1,0:T(8,128)(2,1)S(1)}, bf16[512,128]{1,0:T(8,128)(2,1)S(1)}, u32[]{:S(2)}, u32[]{:S(2)}) collective-permute-start(bf16[512,128]{1,0:T(8,128)(2,1)S(1)} %get-tuple-element.27), channel_id=1, source_target_pairs={{0,24},{8,0},{16,8},{24,16},{1,25},{9,1},{17,9},{25,17},{2,26},{10... | collective-permute-start | bytes 393224 | tf_op jit(solution)/shard_map/ppermute | solution.py:175
  152.5 3.4 %collective-permute-done.17 = bf16[512,128]{1,0:T(8,128)(2,1)S(1)} collective-permute-done((bf16[512,128]{1,0:T(8,128)(2,1)S(1)}, bf16[512,128]{1,0:T(8,128)(2,1)S(1)}, u32[]{:S(2)}, u32[]{:S(2)}) %collective-permute-start.17) | collective-permute-done | bytes 131104 | tf_op jit(solution)/shard_map/ppermute | solution.py:175
  157.1 1.7 %reduce_sum.12 = bf16[32,896]{1,0:T(8,128)(2,1)} reduce(bf16[8,32,896]{2,1,0:T(8,128)(2,1)} %all-to-all-done.2, bf16[]{:T(256)} %constant.22.clone.1), dimensions={0}, to_apply=%region_0.1 | reduce | flops 200704 | bytes 516098 | tf_op jit(solution)/shard_map/reduce_sum | solution.py:225
  (80 shorter events, 20.2 us)
Async XLA Ops:
  17.4 50.3 %all-to-all-start = ((bf16[8,4,128,128]{3,2,1,0:T(8,128)(2,1)}), bf16[8,4,128,128]{3,2,1,0:T(8,128)(2,1)S(1)}, u32[]{:S(2)}, u32[]{:S(2)}) async-start(bf16[8,4,128,128]{3,2,1,0:T(8,128)(2,1)} %bitcast_select_fusion), calls=%async_computation | async-start | bytes 2097152 | tf_op jit(solution)/shard_map/all_to_all | solution.py:197
  26.2 76.7 %all-gather.4.cloned.1.call-start = ((), (), s32[]{:S(2)}) async-start(), calls=%async_computation.3 | async-start | bytes 2293760 | tf_op jit(solution)/shard_map/all_gather | solution.py:199
  26.2 13.4 %collective-permute-start = (bf16[8,128,256]{2,1,0:T(8,128)(2,1)S(1)}, bf16[8,128,256]{2,1,0:T(8,128)(2,1)}, u32[]{:S(2)}, u32[]{:S(2)}) collective-permute-start(bf16[8,128,256]{2,1,0:T(8,128)(2,1)S(1)} %bitcast.39), channel_id=1, source_target_pairs={{0,192},{64,0},{128,64},{192,128},{1,193},{65,1},{129,65},{193,129... | collective-permute-start | bytes 1572872 | tf_op jit(solution)/shard_map/ppermute | solution.py:175
  28.9 16.1 %collective-permute-start.1 = (bf16[8,128,256]{2,1,0:T(8,128)(2,1)S(1)}, bf16[8,128,256]{2,1,0:T(8,128)(2,1)}, u32[]{:S(2)}, u32[]{:S(2)}) collective-permute-start(bf16[8,128,256]{2,1,0:T(8,128)(2,1)S(1)} %bitcast.40), channel_id=1, source_target_pairs={{0,64},{64,128},{128,192},{192,0},{1,65},{65,129},{129,193},{193,1... | collective-permute-start | bytes 1572872 | tf_op jit(solution)/shard_map/ppermute | solution.py:175
  28.9 29.5 %collective-permute-start.2 = (bf16[8,128,256]{2,1,0:T(8,128)(2,1)S(1)}, bf16[8,128,256]{2,1,0:T(8,128)(2,1)}, u32[]{:S(2)}, u32[]{:S(2)}) collective-permute-start(bf16[8,128,256]{2,1,0:T(8,128)(2,1)S(1)} %bitcast.41), channel_id=1, source_target_pairs={{0,32},{32,0},{1,33},{33,1},{2,34},{34,2},{3,35},{35,3},{4,36},{36... | collective-permute-start | bytes 1572872 | tf_op jit(solution)/shard_map/ppermute | solution.py:175
  41.2 9.9 %collective-permute-start.5 = (bf16[4,128,256]{2,1,0:T(8,128)(2,1)}, bf16[4,128,256]{2,1,0:T(8,128)(2,1)}, u32[]{:S(2)}, u32[]{:S(2)}) collective-permute-start(bf16[4,128,256]{2,1,0:T(8,128)(2,1)} %slice.8), channel_id=1, source_target_pairs={{0,192},{64,0},{128,64},{192,128},{1,193},{65,1},{129,65},{193,129... | collective-permute-start | bytes 786440 | tf_op jit(solution)/shard_map/ppermute | solution.py:175
  46.7 7.9 %collective-permute-start.6 = (bf16[4,128,256]{2,1,0:T(8,128)(2,1)}, bf16[4,128,256]{2,1,0:T(8,128)(2,1)}, u32[]{:S(2)}, u32[]{:S(2)}) collective-permute-start(bf16[4,128,256]{2,1,0:T(8,128)(2,1)} %slice.9), channel_id=1, source_target_pairs={{0,64},{64,128},{128,192},{192,0},{1,65},{65,129},{129,193},{193,1... | collective-permute-start | bytes 786440 | tf_op jit(solution)/shard_map/ppermute | solution.py:175
  46.7 11.7 %collective-permute-start.3 = (bf16[8,128,256]{2,1,0:T(8,128)(2,1)}, bf16[8,128,256]{2,1,0:T(8,128)(2,1)}, u32[]{:S(2)}, u32[]{:S(2)}) collective-permute-start(bf16[8,128,256]{2,1,0:T(8,128)(2,1)} %collective-permute-done.refs_1_), channel_id=1, source_target_pairs={{0,32},{32,0},{1,33},{33,1},{2,34},{34,2},{3,35},{35,3},{4,36},{36... | collective-permute-start | bytes 1572872 | tf_op jit(solution)/shard_map/ppermute | solution.py:175
  46.7 11.7 %collective-permute-start.4 = (bf16[8,128,256]{2,1,0:T(8,128)(2,1)}, bf16[8,128,256]{2,1,0:T(8,128)(2,1)}, u32[]{:S(2)}, u32[]{:S(2)}) collective-permute-start(bf16[8,128,256]{2,1,0:T(8,128)(2,1)} %collective-permute-done.1.refs_2_), channel_id=1, source_target_pairs={{0,32},{32,0},{1,33},{33,1},{2,34},{34,2},{3,35},{35,3},{4,36},{36... | collective-permute-start | bytes 1572872 | tf_op jit(solution)/shard_map/ppermute | solution.py:175
  51.1 7.3 %collective-permute-start.7 = (bf16[4,128,256]{2,1,0:T(8,128)(2,1)}, bf16[4,128,256]{2,1,0:T(8,128)(2,1)S(1)}, u32[]{:S(2)}, u32[]{:S(2)}) collective-permute-start(bf16[4,128,256]{2,1,0:T(8,128)(2,1)} %collective-permute-done.5.refs_6_), channel_id=1, source_target_pairs={{0,32},{32,0},{1,33},{33,1},{2,34},{34,2},{3,35},{35,3},{4,36},{36... | collective-permute-start | bytes 786440 | tf_op jit(solution)/shard_map/ppermute | solution.py:175
  67.8 35.1 %all-to-all-start.1 = ((bf16[32,4,32,256]{3,2,1,0:T(8,128)(2,1)}), bf16[32,4,32,256]{3,2,1,0:T(8,128)(2,1)}, u32[]{:S(2)}, u32[]{:S(2)}) async-start(bf16[32,4,32,256]{3,2,1,0:T(8,128)(2,1)} %bitcast.46), calls=%async_computation.1 | async-start | bytes 4194304 | tf_op jit(solution)/shard_map/all_to_all | solution.py:213
  73.0 62.9 %collective-permute-start.16 = (bf16[8,4,128,128]{3,2,1,0:T(8,128)(2,1)S(1)}, bf16[8,4,128,128]{3,2,1,0:T(8,128)(2,1)}, u32[]{:S(2)}, u32[]{:S(2)}) collective-permute-start(bf16[8,4,128,128]{3,2,1,0:T(8,128)(2,1)S(1)} %all-to-all-done.refs_8_), channel_id=1, source_target_pairs={{0,32},{32,0},{1,33},{33,1},{2,34},{34,2},{3,35},{35,3},{4,36},{36... | collective-permute-start | bytes 3145736 | tf_op jit(solution)/shard_map/ppermute | solution.py:175
  73.3 6.3 %collective-permute-start.20 = (bf16[512,128]{1,0:T(8,128)(2,1)S(1)}, bf16[512,128]{1,0:T(8,128)(2,1)S(1)}, u32[]{:S(2)}, u32[]{:S(2)}) collective-permute-start(bf16[512,128]{1,0:T(8,128)(2,1)S(1)} %copy-done.5), channel_id=1, source_target_pairs={{0,7},{1,0},{2,1},{3,2},{4,3},{5,4},{6,5},{7,6},{8,15},{9,8},{10,9... | collective-permute-start | bytes 393224 | tf_op jit(solution)/shard_map/ppermute | solution.py:175
  73.9 8.4 %collective-permute-start.9 = (bf16[512,128]{1,0:T(8,128)(2,1)S(1)}, bf16[512,128]{1,0:T(8,128)(2,1)S(1)}, u32[]{:S(2)}, u32[]{:S(2)}) collective-permute-start(bf16[512,128]{1,0:T(8,128)(2,1)S(1)} %copy-done.3), channel_id=1, source_target_pairs={{0,7},{1,0},{2,1},{3,2},{4,3},{5,4},{6,5},{7,6},{8,15},{9,8},{10,9... | collective-permute-start | bytes 393224 | tf_op jit(solution)/shard_map/ppermute | solution.py:175
  76.5 8.2 %collective-permute-start.24 = (bf16[512,128]{1,0:T(8,128)(2,1)S(1)}, bf16[512,128]{1,0:T(8,128)(2,1)}, u32[]{:S(2)}, u32[]{:S(2)}) collective-permute-start(bf16[512,128]{1,0:T(8,128)(2,1)S(1)} %copy-done.5), channel_id=1, source_target_pairs={{0,1},{1,2},{2,3},{3,4},{4,5},{5,6},{6,7},{7,0},{8,9},{9,10},{10,1... | collective-permute-start | bytes 393224 | tf_op jit(solution)/shard_map/ppermute | solution.py:175
  81.0 36.8 %collective-permute-start.13 = (bf16[512,128]{1,0:T(8,128)(2,1)S(1)}, bf16[512,128]{1,0:T(8,128)(2,1)S(1)}, u32[]{:S(2)}, u32[]{:S(2)}) collective-permute-start(bf16[512,128]{1,0:T(8,128)(2,1)S(1)} %copy-done.3), channel_id=1, source_target_pairs={{0,1},{1,2},{2,3},{3,4},{4,5},{5,6},{6,7},{7,0},{8,9},{9,10},{10,1... | collective-permute-start | bytes 393224 | tf_op jit(solution)/shard_map/ppermute | solution.py:175
  82.3 37.0 %collective-permute-start.10 = (bf16[512,128]{1,0:T(8,128)(2,1)S(1)}, bf16[512,128]{1,0:T(8,128)(2,1)}, u32[]{:S(2)}, u32[]{:S(2)}) collective-permute-start(bf16[512,128]{1,0:T(8,128)(2,1)S(1)} %collective-permute-done.9.refs_1_), channel_id=1, source_target_pairs={{0,7},{1,0},{2,1},{3,2},{4,3},{5,4},{6,5},{7,6},{8,15},{9,8},{10,9... | collective-permute-start | bytes 393224 | tf_op jit(solution)/shard_map/ppermute | solution.py:175
  84.7 35.2 %collective-permute-start.25 = (bf16[512,128]{1,0:T(8,128)(2,1)}, bf16[512,128]{1,0:T(8,128)(2,1)}, u32[]{:S(2)}, u32[]{:S(2)}) collective-permute-start(bf16[512,128]{1,0:T(8,128)(2,1)} %collective-permute-done.24.refs_7_), channel_id=1, source_target_pairs={{0,1},{1,2},{2,3},{3,4},{4,5},{5,6},{6,7},{7,0},{8,9},{9,10},{10,1... | collective-permute-start | bytes 393224 | tf_op jit(solution)/shard_map/ppermute | solution.py:175
  85.3 36.0 %collective-permute-start.22 = (bf16[512,128]{1,0:T(8,128)(2,1)}, bf16[512,128]{1,0:T(8,128)(2,1)}, u32[]{:S(2)}, u32[]{:S(2)}) collective-permute-start(bf16[512,128]{1,0:T(8,128)(2,1)} %collective-permute-done.21.refs_2_), channel_id=1, source_target_pairs={{0,7},{1,0},{2,1},{3,2},{4,3},{5,4},{6,5},{7,6},{8,15},{9,8},{10,9... | collective-permute-start | bytes 393224 | tf_op jit(solution)/shard_map/ppermute | solution.py:175
  110.6 46.4 %all-to-all-start.2 = ((bf16[8,32,896]{2,1,0:T(8,128)(2,1)}), bf16[8,32,896]{2,1,0:T(8,128)(2,1)}, u32[]{:S(2)}, u32[]{:S(2)}) async-start(bf16[8,32,896]{2,1,0:T(8,128)(2,1)} %bitcast.19), calls=%async_computation.2 | async-start | bytes 917504 | tf_op jit(solution)/shard_map/all_to_all | solution.py:224
  117.9 14.2 %collective-permute-start.14 = (bf16[512,128]{1,0:T(8,128)(2,1)S(1)}, bf16[512,128]{1,0:T(8,128)(2,1)S(1)}, u32[]{:S(2)}, u32[]{:S(2)}) collective-permute-start(bf16[512,128]{1,0:T(8,128)(2,1)S(1)} %collective-permute-done.13.refs_7_), channel_id=1, source_target_pairs={{0,1},{1,2},{2,3},{3,4},{4,5},{5,6},{6,7},{7,0},{8,9},{9,10},{10,1... | collective-permute-start | bytes 393224 | tf_op jit(solution)/shard_map/ppermute | solution.py:175
  119.3 14.2 %collective-permute-start.11 = (bf16[512,128]{1,0:T(8,128)(2,1)}, bf16[512,128]{1,0:T(8,128)(2,1)S(1)}, u32[]{:S(2)}, u32[]{:S(2)}) collective-permute-start(bf16[512,128]{1,0:T(8,128)(2,1)} %collective-permute-done.10.refs_2_), channel_id=1, source_target_pairs={{0,7},{1,0},{2,1},{3,2},{4,3},{5,4},{6,5},{7,6},{8,15},{9,8},{10,9... | collective-permute-start | bytes 393224 | tf_op jit(solution)/shard_map/ppermute | solution.py:175
  119.9 15.6 %collective-permute-start.26 = (bf16[512,128]{1,0:T(8,128)(2,1)}, bf16[512,128]{1,0:T(8,128)(2,1)S(1)}, u32[]{:S(2)}, u32[]{:S(2)}) collective-permute-start(bf16[512,128]{1,0:T(8,128)(2,1)} %collective-permute-done.25.refs_6_), channel_id=1, source_target_pairs={{0,1},{1,2},{2,3},{3,4},{4,5},{5,6},{6,7},{7,0},{8,9},{9,10},{10,1... | collective-permute-start | bytes 393224 | tf_op jit(solution)/shard_map/ppermute | solution.py:175
  121.4 14.5 %collective-permute-start.23 = (bf16[512,128]{1,0:T(8,128)(2,1)}, bf16[512,128]{1,0:T(8,128)(2,1)S(1)}, u32[]{:S(2)}, u32[]{:S(2)}) collective-permute-start(bf16[512,128]{1,0:T(8,128)(2,1)} %collective-permute-done.22.refs_3_), channel_id=1, source_target_pairs={{0,7},{1,0},{2,1},{3,2},{4,3},{5,4},{6,5},{7,6},{8,15},{9,8},{10,9... | collective-permute-start | bytes 393224 | tf_op jit(solution)/shard_map/ppermute | solution.py:175
  132.1 13.1 %collective-permute-start.15 = (bf16[512,128]{1,0:T(8,128)(2,1)S(1)}, bf16[512,128]{1,0:T(8,128)(2,1)S(1)}, u32[]{:S(2)}, u32[]{:S(2)}) collective-permute-start(bf16[512,128]{1,0:T(8,128)(2,1)S(1)} %collective-permute-done.14.refs_6_), channel_id=1, source_target_pairs={{0,1},{1,2},{2,3},{3,4},{4,5},{5,6},{6,7},{7,0},{8,9},{9,10},{10,1... | collective-permute-start | bytes 393224 | tf_op jit(solution)/shard_map/ppermute | solution.py:175
  133.5 11.8 %collective-permute-start.12 = (bf16[512,128]{1,0:T(8,128)(2,1)S(1)}, bf16[512,128]{1,0:T(8,128)(2,1)S(1)}, u32[]{:S(2)}, u32[]{:S(2)}) collective-permute-start(bf16[512,128]{1,0:T(8,128)(2,1)S(1)} %collective-permute-done.11.refs_3_), channel_id=1, source_target_pairs={{0,7},{1,0},{2,1},{3,2},{4,3},{5,4},{6,5},{7,6},{8,15},{9,8},{10,9... | collective-permute-start | bytes 393224 | tf_op jit(solution)/shard_map/ppermute | solution.py:175
  139.6 9.9 %collective-permute-start.27 = (bf16[512,128]{1,0:T(8,128)(2,1)S(1)}, bf16[512,128]{1,0:T(8,128)(2,1)S(1)}, u32[]{:S(2)}, u32[]{:S(2)}) collective-permute-start(bf16[512,128]{1,0:T(8,128)(2,1)S(1)} %get-tuple-element.30), channel_id=1, source_target_pairs={{0,8},{8,16},{16,24},{24,0},{1,9},{9,17},{17,25},{25,1},{2,10},{10... | collective-permute-start | bytes 393224 | tf_op jit(solution)/shard_map/ppermute | solution.py:175
  141.3 10.5 %collective-permute-start.28 = (bf16[512,128]{1,0:T(8,128)(2,1)S(1)}, bf16[512,128]{1,0:T(8,128)(2,1)S(1)}, u32[]{:S(2)}, u32[]{:S(2)}) collective-permute-start(bf16[512,128]{1,0:T(8,128)(2,1)S(1)} %get-tuple-element.31), channel_id=1, source_target_pairs={{0,16},{8,24},{16,0},{24,8},{1,17},{9,25},{17,1},{25,9},{2,18},{10... | collective-permute-start | bytes 393224 | tf_op jit(solution)/shard_map/ppermute | solution.py:175
  144.4 7.5 %collective-permute-start.29 = (bf16[512,128]{1,0:T(8,128)(2,1)S(1)}, bf16[512,128]{1,0:T(8,128)(2,1)S(1)}, u32[]{:S(2)}, u32[]{:S(2)}) collective-permute-start(bf16[512,128]{1,0:T(8,128)(2,1)S(1)} %get-tuple-element.32), channel_id=1, source_target_pairs={{0,24},{8,0},{16,8},{24,16},{1,25},{9,1},{17,9},{25,17},{2,26},{10... | collective-permute-start | bytes 393224 | tf_op jit(solution)/shard_map/ppermute | solution.py:175
  147.8 8.1 %collective-permute-start.17 = (bf16[512,128]{1,0:T(8,128)(2,1)S(1)}, bf16[512,128]{1,0:T(8,128)(2,1)S(1)}, u32[]{:S(2)}, u32[]{:S(2)}) collective-permute-start(bf16[512,128]{1,0:T(8,128)(2,1)S(1)} %get-tuple-element.25), channel_id=1, source_target_pairs={{0,8},{8,16},{16,24},{24,0},{1,9},{9,17},{17,25},{25,1},{2,10},{10... | collective-permute-start | bytes 393224 | tf_op jit(solution)/shard_map/ppermute | solution.py:175
  149.0 6.9 %collective-permute-start.18 = (bf16[512,128]{1,0:T(8,128)(2,1)S(1)}, bf16[512,128]{1,0:T(8,128)(2,1)S(1)}, u32[]{:S(2)}, u32[]{:S(2)}) collective-permute-start(bf16[512,128]{1,0:T(8,128)(2,1)S(1)} %get-tuple-element.26), channel_id=1, source_target_pairs={{0,16},{8,24},{16,0},{24,8},{1,17},{9,25},{17,1},{25,9},{2,18},{10... | collective-permute-start | bytes 393224 | tf_op jit(solution)/shard_map/ppermute | solution.py:175
  149.5 6.8 %collective-permute-start.19 = (bf16[512,128]{1,0:T(8,128)(2,1)S(1)}, bf16[512,128]{1,0:T(8,128)(2,1)S(1)}, u32[]{:S(2)}, u32[]{:S(2)}) collective-permute-start(bf16[512,128]{1,0:T(8,128)(2,1)S(1)} %get-tuple-element.27), channel_id=1, source_target_pairs={{0,24},{8,0},{16,8},{24,16},{1,25},{9,1},{17,9},{25,17},{2,26},{10... | collective-permute-start | bytes 393224 | tf_op jit(solution)/shard_map/ppermute | solution.py:175
  (12 other events, 62.0 us)
Sparse Core Ops, SparseCore 0:
  29.1 32.8 all-gather.3
